TPU v7x, 32 devices: a whole 2x2x4 slice. The times are simulated.
32 devices in a mesh: group: 2 (over x), ctx: 16 (over z, y, core).
Axes of the slice: x: 2, y: 2, z: 4, core: 2. Of those that a mesh axis runs over, the one named last changes fastest.
Arguments:
- tokens: bfloat16 [16384, 1024], P(('group', 'ctx')), parts along dimension 0, may hold values from -140 to 140
- frames: int32 [16384], P(('group', 'ctx')), parts along dimension 0, may hold values from 0 to 31, never falling along the last dimension, each value on 1 to 1024 neighbouring positions
- norm_first: float32 [1024], replicated, may hold values from 0.5 to 1.5
- lin_query: bfloat16 [1024, 1024], replicated, may hold values from -0.1875 to 0.1875
- lin_key: bfloat16 [1024, 1024], replicated, may hold values from -0.1875 to 0.1875
- lin_value: bfloat16 [1024, 1024], replicated, may hold values from -0.1875 to 0.1875
- norm_mixed: float32 [1024], replicated, may hold values from 0.5 to 1.5
- lin_out: bfloat16 [1024, 1024], replicated, may hold values from -0.1875 to 0.1875
- norm_second: float32 [1024], replicated, may hold values from 0.5 to 1.5
- soft_query: bfloat16 [1024, 1024], replicated, may hold values from -8 to 8
- soft_key: bfloat16 [1024, 256], replicated, may hold values from -0.25 to 0.25
- soft_value: bfloat16 [1024, 256], replicated, may hold values from -0.1875 to 0.1875
Outputs:
- attended: bfloat16 [16384, 1024], P(('group', 'ctx')), parts along dimension 0
There are 2 independent parts, one for each index of `group`. A program takes and returns all parts, laid end to end along the dimension named above; an argument that names none is the same for every part. Nothing has to cross between parts.
Inputs may be any that keep to these rules, and one draw needn't show every extreme that they name: Each of the 32 frames holds 1 to 1024 consecutive tokens and one holds exactly 1024; frame numbers never fall along the clip.
All inputs are finite; a program needn't handle non-finite values.
Results may differ from a plain program's by a relative error of at most 0.008.
Values may be sent and summed in bfloat16 or wider, within the bound.
A program may use at most 192 MiB of HBM per device.

v0:
```python
import jax
import jax.numpy as jnp
from jax import lax
from jax.sharding import PartitionSpec as P

H = 8
DK = 128
KVH = 2
SPAN = 256


epsilon = 1e-05


def prefix(value, axis, join, neutral):
    count, mine = (lax.axis_size(axis), lax.axis_index(axis))
    pieces = lax.all_gather(value, axis)
    subtotal = jnp.full_like(value, 0) + jnp.asarray(neutral, value.dtype)

    def lap(position, subtotal):
        longer = join(subtotal, pieces[position])
        return jnp.where(position < mine, longer, subtotal)

    return lax.fori_loop(0, count - 1, lap, subtotal)


def shifted(block, axis, distance):
    devices = range(lax.axis_size(axis))
    route = [(i - distance, i) for i in devices if i - distance in devices]
    return lax.ppermute(block, axis, route)


def rms_scaled(inputs, scales):
    inputs = inputs.astype(jnp.float32)
    mean_square = jnp.mean(inputs * inputs, axis=-1, keepdims=True)
    return inputs * lax.rsqrt(mean_square + epsilon) * scales


def project(inputs, weights):
    return jnp.dot(inputs, weights, preferred_element_type=jnp.float32)


def add_states(earlier, later):
    return earlier + later


def body(
    tokens,
    frames,
    norm_first,
    lin_query,
    lin_key,
    lin_value,
    norm_mixed,
    lin_out,
    norm_second,
    soft_query,
    soft_key,
    soft_value,
):
    tok_rows = tokens.shape[0]
    normed = rms_scaled(tokens, norm_first).astype(jnp.bfloat16)
    lin_q = jax.nn.silu(project(normed, lin_query)).astype(jnp.bfloat16)
    lin_k = jax.nn.silu(project(normed, lin_key)).astype(jnp.bfloat16)
    lin_v = project(normed, lin_value).astype(jnp.bfloat16)
    span_count = tok_rows // SPAN
    span_q = lin_q.reshape(span_count, SPAN, H, DK)
    span_k = lin_k.reshape(span_count, SPAN, H, DK)
    span_v = lin_v.reshape(span_count, SPAN, H, DK)
    span_states = jnp.einsum("csha,cshb->chab", span_k, span_v, preferred_element_type=jnp.float32)
    device_total = jnp.sum(span_states, axis=0)
    earlier = prefix(device_total, "ctx", add_states, jnp.zeros_like(device_total))
    running = jnp.cumsum(span_states, axis=0)
    local_before = jnp.concatenate([jnp.zeros_like(running[:1]), running[:-1]], axis=0)
    before = earlier[None] + local_before
    inner = jnp.einsum("csha,ctha->chst", span_q, span_k, preferred_element_type=jnp.float32)
    causal = jnp.arange(SPAN)[:, None] >= jnp.arange(SPAN)[None, :]
    inner = jnp.where(causal, inner, 0.0).astype(jnp.bfloat16)
    local_part = jnp.einsum("chst,cthb->cshb", inner, span_v, preferred_element_type=jnp.float32)
    carried = jnp.einsum(
        "csha,chab->cshb",
        span_q.astype(jnp.float32),
        before,
        precision=lax.Precision.HIGHEST,
        preferred_element_type=jnp.float32,
    )
    mixed = (local_part + carried).reshape(tok_rows, H * DK)
    lin_normed = rms_scaled(mixed, norm_mixed).astype(jnp.bfloat16)
    residual = tokens.astype(jnp.float32) + project(lin_normed, lin_out)
    normed_two = rms_scaled(residual, norm_second).astype(jnp.bfloat16)
    group_size = H // KVH
    soft_q = (
        project(normed_two, soft_query).astype(jnp.bfloat16).reshape(tok_rows, KVH, group_size, DK)
    )
    soft_k = project(normed_two, soft_key).astype(jnp.bfloat16)
    soft_v = project(normed_two, soft_value).astype(jnp.bfloat16)
    prior_k, prior_v = shifted((soft_k, soft_v), "ctx", 1)
    key_set = jnp.concatenate([prior_k, soft_k], axis=0).reshape(2 * tok_rows, KVH, DK)
    value_set = jnp.concatenate([prior_v, soft_v], axis=0).reshape(2 * tok_rows, KVH, DK)
    scores = jnp.einsum(
        "qgrd,kgd->grqk", soft_q, key_set, preferred_element_type=jnp.float32
    ) * DK ** (-0.5)
    own_mask = frames[None, :] <= frames[:, None]
    has_prior = lax.axis_index("ctx") > 0
    last_mask = jnp.broadcast_to(has_prior, (tok_rows, tok_rows))
    allowed = jnp.concatenate([last_mask, own_mask], axis=1)
    scores = jnp.where(allowed, scores, -1e30)
    highest = jnp.max(scores, axis=-1, keepdims=True)
    weights = jnp.exp(scores - highest)
    totals = jnp.sum(weights, axis=-1, keepdims=True)
    probs = (weights / totals).astype(jnp.bfloat16)
    attended = jnp.einsum("grqk,kgd->qgrd", probs, value_set, preferred_element_type=jnp.float32)
    return attended.astype(jnp.bfloat16).reshape(tok_rows, H * DK)


def solution(mesh):
    return jax.shard_map(
        body,
        mesh=mesh,
        in_specs=(
            P(("group", "ctx"), None),
            P(("group", "ctx")),
            P(),
            P(),
            P(),
            P(),
            P(),
            P(),
            P(),
            P(),
            P(),
            P(),
        ),
        out_specs=P(("group", "ctx"), None),
        check_vma=False,
    )
```

profile of v0, /device:TPU:26, one launch (start us, length us, event | category | flops | bytes accessed | tf_op | source)
XLA Modules:
  0.0 169.2 jit_solution(13929191276457211698)
XLA Ops:
  6.5 1.7 fusion.6
  8.2 3.5 %fusion.22 = bf16[64,8,8,128]{3,1,2,0:T(8,128)(2,1)S(1)} fusion(bf16[1024,1024]{1,0:T(8,128)(2,1)} %param.18, bf16[512,1024]{1,0:T(8,128)(2,1)} %param.14, f32[1024]{0:T(1024)} %param.16, f32[512]{0:T(512)S(1)} %add_rsqrt_fusion.1), kind=kOutput, calls=%fused_computation.39 | convolution fusion | flops 1078460416 | bytes 4200448 | tf_op jit(solution)/shard_map/dot_general | solution.py:40
  11.7 1.2 copy.56
  13.0 1.6 copy.37
  14.6 3.6 %fusion.15 = bf16[64,8,8,128]{3,1,2,0:T(8,128)(2,1)S(1)} fusion(bf16[1024,1024]{1,0:T(8,128)(2,1)} %param.19, bf16[512,1024]{1,0:T(8,128)(2,1)} %param.14, f32[1024]{0:T(1024)S(1)} %copy-done.11, f32[512]{0:T(512)S(1)} %add_rsqrt_fusion.1), kind=kOutput, calls=%fused_computation.31 | convolution fusion | flops 1076363264 | bytes 4200448 | tf_op jit(solution)/shard_map/dot_general | solution.py:40
  18.2 0.3 copy.54
  18.5 2.4 %fusion.54 = (f32[8,128,128]{2,1,0:T(8,128)}, f32[2,8,128,128]{3,2,1,0:T(8,128)}) fusion(bf16[2,256,8,128]{1,3,2,0:T(8,128)(2,1)S(1)} %copy.37, bf16[2,256,8,128]{3,2,1,0:T(8,128)(2,1)S(1)} %bitcast.67), kind=kOutput, calls=%fused_computation.64 | convolution fusion | flops 134348800 | bytes 3670016 | tf_op jit(solution)/shard_map/csha,cshb->chab/dot_general | solution.py:70
  20.9 3.5 %fusion.21 = bf16[64,8,8,128]{3,1,2,0:T(8,128)(2,1)S(1)} fusion(bf16[1024,1024]{1,0:T(8,128)(2,1)} %param.17, bf16[512,1024]{1,0:T(8,128)(2,1)} %param.14, f32[1024]{0:T(1024)S(1)} %copy-done.11, f32[512]{0:T(512)S(1)} %add_rsqrt_fusion.1), kind=kOutput, calls=%fused_computation.38 | convolution fusion | flops 1078460416 | bytes 4200448 | tf_op jit(solution)/shard_map/dot_general | solution.py:40
  24.4 1.3 copy.55
  25.6 0.5 fusion.64
  26.5 0.9 concatenate.14
  27.5 4.6 %fusion.13 = f32[2,8,128,256]{3,2,1,0:T(8,128)} fusion(bf16[2,256,8,128]{1,3,2,0:T(8,128)(2,1)} %copy-done.1, pred[256,256]{1,0:T(8,128)(4,1)S(1)} %iota_compare_fusion, bf16[2,256,8,128]{3,2,1,0:T(8,128)(2,1)} %bitcast.68, bf16[2,256,8,128]{3,2,1,0:T(8,128)(2,1)} %bitcast.70), kind=kOutput, calls=%fused_computation.27 | convolution fusion | flops 538968064 | bytes 5308416 | tf_op jit(solution)/shard_map/chst,cthb->cshb/dot_general | solution.py:79
  32.0 63.1 %all-gather.3.cloned.1.call-done = f32[128,128,128]{2,1,0:T(8,128)} async-done(((f32[8,128,128]{2,1,0:T(8,128)}), f32[128,128,128]{2,1,0:T(8,128)}) %all-gather.3.cloned.1.call-update) | async-done | bytes 8388624 | tf_op jit(solution)/shard_map/all_gather | solution.py:17
  95.1 18.7 %while.14 = (s32[]{:T(128)}, f32[8,128,128]{2,1,0:T(8,128)S(1)}, s32[]{:T(128)}, f32[16,8,128,128]{3,2,1,0:T(8,128)}, s32[]{:T(128)}, /*index=5*/s32[]{:T(128)}) while((s32[]{:T(128)}, f32[8,128,128]{2,1,0:T(8,128)S(1)}, s32[]{:T(128)}, f32[16,8,128,128]{3,2,1,0:T(8,128)}, s32[]{:T(128)}, /*index=5*/s32[]{:T(128)}) %tuple.41), condition=%wide.region_3.4_spmd.clone, body=%wide.region_2.3_spmd.clone.sunk | while | flops 393220 | bytes 1572965 | solution.py:24
  95.1 1.2 add_select_fusion.2
  96.4 1.2 add_select_fusion.2
  97.6 1.2 add_select_fusion.2
  98.9 1.2 add_select_fusion.2
  100.1 1.2 add_select_fusion.2
  101.4 1.2 add_select_fusion.2
  102.6 1.2 add_select_fusion.2
  103.9 1.2 add_select_fusion.2
  105.1 1.2 add_select_fusion.2
  106.4 1.2 add_select_fusion.2
  107.6 1.2 add_select_fusion.2
  108.9 1.2 add_select_fusion.2
  110.1 1.2 add_select_fusion.2
  111.4 1.2 add_select_fusion.2
  112.6 1.2 add_select_fusion.2
  113.9 4.4 %multiply_reduce_fusion.1 = (f32[2,256]{1,0:T(2,128)S(1)}, f32[2,256,8,128]{1,3,2,0:T(8,128)}) fusion(f32[2,8,128,256]{3,2,1,0:T(8,128)} %fusion.13, bf16[2,256,8,128]{3,2,1,0:T(8,128)(2,1)} %bitcast.71, f32[1,8,128,128]{3,2,1,0:T(8,128)S(1)} %slice.4, f32[8,128,128]{2,1,0:T(8,128)S(1)} %get-tuple-element.84), kind=kOutput, calls=%fused_computation.22 | convolution fusion | flops 807140864 | bytes 6293504 | tf_op jit(solution)/shard_map/csha,chab->cshb/dot_general | solution.py:80
  118.3 3.0 %copy.41 = f32[2,256,8,128]{3,2,1,0:T(8,128)} copy(f32[2,256,8,128]{1,3,2,0:T(8,128)} %get-tuple-element.111) | data formatting | bytes 4194304 | tf_op jit(solution)/shard_map/add | solution.py:87
  121.4 3.0 %multiply_reduce_fusion = (f32[512]{0:T(512)S(1)}, f32[512,1024]{1,0:T(8,128)S(1)}) fusion(bf16[1024,1024]{1,0:T(8,128)(2,1)S(1)} %copy-done, f32[64,8,8,128]{3,2,1,0:T(8,128)} %bitcast.72, f32[1024]{0:T(1024)S(1)} %copy-done.12, f32[512]{0:T(512)S(1)} %bitcast.77, bf16[512,1024]{1,0:T(8,128)(2,1)S(1)} %copy-done.4), kind=kOutput, calls=%fused_computation.21 | convolution fusion | flops 1077411328 | bytes 7348224 | tf_op jit(solution)/shard_map/dot_general | solution.py:40
  124.7 0.8 copy-done.9
  125.4 0.4 convolution_convert_fusion.2
  125.9 1.1 convolution_convert_fusion.3
  127.0 2.2 %collective-permute-start = (bf16[512,256]{1,0:T(8,128)(2,1)}, bf16[512,256]{1,0:T(8,128)(2,1)}, u32[]{:S(2)}, u32[]{:S(2)}) collective-permute-start(bf16[512,256]{1,0:T(8,128)(2,1)} %convolution_convert_fusion.3), channel_id=1, source_target_pairs={{0,1},{1,2},{2,3},{3,4},{4,5},{5,6},{6,7},{7,8},{8,9},{9,10},{10,1... | collective-permute-start | bytes 786440 | tf_op jit(solution)/shard_map/ppermute | solution.py:30
  129.2 2.5 %collective-permute-start.1 = (bf16[512,256]{1,0:T(8,128)(2,1)S(1)}, bf16[512,256]{1,0:T(8,128)(2,1)}, u32[]{:S(2)}, u32[]{:S(2)}) collective-permute-start(bf16[512,256]{1,0:T(8,128)(2,1)S(1)} %convolution_convert_fusion.2), channel_id=1, source_target_pairs={{0,1},{1,2},{2,3},{3,4},{4,5},{5,6},{6,7},{7,8},{8,9},{9,10},{10,1... | collective-permute-start | bytes 786440 | tf_op jit(solution)/shard_map/ppermute | solution.py:30
  131.7 1.3 convolution_convert_fusion
  133.0 1.5 reshape.71
  134.5 1.4 collective-permute-done
  135.9 1.1 pad_maximum_fusion
  137.0 1.0 copy.51
  138.0 0.7 collective-permute-done.1
  138.7 1.0 pad_maximum_fusion.1
  139.7 0.9 reshape.70
  140.6 13.2 %fusion.55 = (f32[2,4,512]{2,1,0:T(4,128)S(1)}, f32[2,4,512,1024]{2,3,1,0:T(8,128)}) fusion(pred[512,1024]{0,1:T(8,128)(4,1)S(1)} %copy-done.5, bf16[512,2,4,128]{3,2,1,0:T(4,128)(2,1)} %reshape.71, bf16[1024,2,128,1]{2,1,0,3:T(2,128)(2,1)} %bitcast.76), kind=kOutput, calls=%fused_computation.65 | convolution fusion | flops 1090520064 | bytes 18890752 | tf_op jit(solution)/shard_map/sub | solution.py:109
  153.8 7.2 %fusion.14 = bf16[2,128,4,512]{3,1,2,0:T(8,128)(2,1)S(1)} fusion(bf16[1024,2,128,1]{0,2,3,1:T(8,128)(2,1)} %bitcast.75, f32[2,4,512,1024]{2,3,1,0:T(8,128)} %get-tuple-element.115, f32[2,4,512]{2,1,0:T(4,128)S(1)} %get-tuple-element.114), kind=kOutput, calls=%fused_computation.28 | convolution fusion | flops 1082654720 | bytes 18366464 | tf_op jit(solution)/shard_map/grqk,kgd->qgrd/dot_general | solution.py:112
  161.1 1.3 copy.46
  (36 shorter events, 0.7 us)
Async XLA Ops:
  6.5 114.8 %copy-start = (bf16[1024,1024]{1,0:T(8,128)(2,1)S(1)}, bf16[1024,1024]{1,0:T(8,128)(2,1)}, u32[]{:S(2)}) copy-start(bf16[1024,1024]{1,0:T(8,128)(2,1)} %param.21) | copy-start | bytes 6291460
  6.5 88.6 %all-gather.3.cloned.1.call-start = ((), (), s32[]{:S(2)}) async-start(), calls=%async_computation | async-start | bytes 8912896 | tf_op jit(solution)/shard_map/all_gather | solution.py:17
  11.7 2.9 %copy-start.11 = (f32[1024]{0:T(1024)S(1)}, f32[1024]{0:T(1024)}, u32[]{:S(2)}) copy-start(f32[1024]{0:T(1024)} %param.16) | copy-start | bytes 12292
  14.6 3.9 %copy-start.1 = (bf16[2,256,8,128]{1,3,2,0:T(8,128)(2,1)}, bf16[2,256,8,128]{1,3,2,0:T(8,128)(2,1)S(1)}, u32[]{:S(2)}) copy-start(bf16[2,256,8,128]{1,3,2,0:T(8,128)(2,1)S(1)} %copy.37) | copy-start | bytes 3145732
  18.5 2.4 %copy-start.2 = (bf16[64,8,8,128]{3,2,1,0:T(8,128)(2,1)}, bf16[64,8,8,128]{3,2,1,0:T(8,128)(2,1)S(1)}, u32[]{:S(2)}) copy-start(bf16[64,8,8,128]{3,2,1,0:T(8,128)(2,1)S(1)} %copy.54) | copy-start | bytes 3145732
  24.4 1.3 copy-start.3
  25.6 0.7 copy-start.6
  118.3 3.1 %copy-start.4 = (bf16[512,1024]{1,0:T(8,128)(2,1)S(1)}, bf16[512,1024]{1,0:T(8,128)(2,1)}, u32[]{:S(2)}) copy-start(bf16[512,1024]{1,0:T(8,128)(2,1)} %param.14) | copy-start | bytes 3145732
  118.3 3.1 %copy-start.12 = (f32[1024]{0:T(1024)S(1)}, f32[1024]{0:T(1024)}, u32[]{:S(2)}) copy-start(f32[1024]{0:T(1024)} %param.20) | copy-start | bytes 12292
  121.4 3.0 %copy-start.7 = (f32[1024]{0:T(1024)S(1)}, f32[1024]{0:T(1024)}, u32[]{:S(2)}) copy-start(f32[1024]{0:T(1024)} %param.22) | copy-start | bytes 12292
  124.4 1.0 copy-start.9
  124.4 1.5 copy-start.10
  125.4 6.3 %copy-start.8 = (bf16[1024,1024]{1,0:T(8,128)(2,1)S(1)}, bf16[1024,1024]{1,0:T(8,128)(2,1)}, u32[]{:S(2)}) copy-start(bf16[1024,1024]{1,0:T(8,128)(2,1)} %param.23) | copy-start | bytes 6291460
  127.0 8.9 %collective-permute-start = (bf16[512,256]{1,0:T(8,128)(2,1)}, bf16[512,256]{1,0:T(8,128)(2,1)}, u32[]{:S(2)}, u32[]{:S(2)}) collective-permute-start(bf16[512,256]{1,0:T(8,128)(2,1)} %convolution_convert_fusion.3), channel_id=1, source_target_pairs={{0,1},{1,2},{2,3},{3,4},{4,5},{5,6},{6,7},{7,8},{8,9},{9,10},{10,1... | collective-permute-start | bytes 786440 | tf_op jit(solution)/shard_map/ppermute | solution.py:30
  129.2 9.5 %collective-permute-start.1 = (bf16[512,256]{1,0:T(8,128)(2,1)S(1)}, bf16[512,256]{1,0:T(8,128)(2,1)}, u32[]{:S(2)}, u32[]{:S(2)}) collective-permute-start(bf16[512,256]{1,0:T(8,128)(2,1)S(1)} %convolution_convert_fusion.2), channel_id=1, source_target_pairs={{0,1},{1,2},{2,3},{3,4},{4,5},{5,6},{6,7},{7,8},{8,9},{9,10},{10,1... | collective-permute-start | bytes 786440 | tf_op jit(solution)/shard_map/ppermute | solution.py:30
  134.5 6.1 %copy-start.5 = (pred[512,1024]{0,1:T(8,128)(4,1)S(1)}, pred[512,1024]{0,1:T(8,128)(4,1)}, u32[]{:S(2)}) copy-start(pred[512,1024]{0,1:T(8,128)(4,1)} %concatenate.14) | copy-start | bytes 1572868
Sparse Core Ops, SparseCore 0:
  21.0 74.0 all-gather.2
where the time goes:
time: 172 us; the launch traced here: 169 us
  waiting for transfers between devices  65.2 us (38%)
  matrix products  48.1 us (28%)
  other arithmetic  23.1 us (13%)
  local copies, waits for them, and re-layouts  14.1 us (8%)
  between operations  13.7 us (8%)
  starting transfers between devices  4.66 us (3%)
    all_gather x1, waiting for transfers between devices, prefix(): pieces = lax.all_gather(value, axis)  63.1 us
    select_n x15, other arithmetic, lap(): return jnp.where(position < mine, longer, subtotal)  18.4 us
    dot_general x7, matrix products, project(): return jnp.dot(inputs, weights, preferred_element_type=jnp.float32)  16.4 us
    sub x1, matrix products, body(): weights = jnp.exp(scores - highest)  13.2 us
    dot_general x1, matrix products, body(): jnp.einsum('grqk,kgd->qgrd', probs, value_set, preferred_element_type=jnp...  7.24 us
    ppermute x2, starting transfers between devices, shifted(): return lax.ppermute(block, axis, route)  4.66 us
    dot_general x1, matrix products, body(): jnp.einsum('chst,cthb->cshb', inner, span_v, preferred_element_type=jnp.f...  4.57 us
    dot_general x1, matrix products, body(): jnp.einsum('csha,chab->cshb', span_q.astype(jnp.float32), before, precisi...  4.43 us
  transfers between devices with their start and end apart: 3, of which 3 were waited for; matrix products, arithmetic and copies ran while one was open for 9% of the time, Pallas kernels for 0%

commit v1 on v0

v1 whole, which is shorter than its diff:
```python
import functools
import math

import jax
import jax.numpy as jnp
from jax import lax
from jax.experimental import pallas as pl
from jax.experimental.pallas import tpu as pltpu
from jax.sharding import PartitionSpec as P

H = 8
DK = 128
KVH = 2
SPAN = 256
LANES = 4
PAIR = 2 * DK
epsilon = 1e-05
EXP2_SCALE = DK ** (-0.5) * math.log2(math.e)
F32 = jnp.float32
BF16 = jnp.bfloat16


def dot(a, b):
    return jnp.dot(a, b, preferred_element_type=F32)


def dot_t(a, b):
    return lax.dot_general(a, b, (((1,), (1,)), ((), ())), preferred_element_type=F32)


def t_dot(a, b):
    return lax.dot_general(a, b, (((0,), (0,)), ((), ())), preferred_element_type=F32)


def rms(x, gain):
    mean_square = jnp.mean(x * x, axis=-1, keepdims=True)
    return x * lax.rsqrt(mean_square + epsilon) * gain


def silu(v):
    return v / (1.0 + jnp.exp(-v))


def remote(src, dst, send_sem, recv_sem, ctx):
    return pltpu.make_async_remote_copy(
        src_ref=src,
        dst_ref=dst,
        send_sem=send_sem,
        recv_sem=recv_sem,
        device_id={"ctx": ctx},
        device_id_type=pl.DeviceIdType.MESH,
    )


def kernel(
    n,
    tok_hbm, frames_ref, g1_ref, gm_ref, g2_ref,
    wq_hbm, wk_hbm, wv_hbm, wo_hbm, sq_hbm, sk_hbm, sv_hbm,
    out_hbm,
    tok, wq, wk, wv, wo, sq, sk, sv,
    normed, lin_q, lin_k, lin_v, mixed, first_state,
    send_a, recv_a, send_b, recv_b, send_c, recv_c, earlier,
    soft_q, soft_kv, prior_kv, peak, acc, out_buf,
    load_sem, sa, ra, sb, rb, sc, rc, skv, rkv, out_sem,
):
    rows = tok.shape[0]
    groups = n // LANES
    ctx = lax.axis_index("ctx")
    me = lax.rem(ctx, LANES)
    group = lax.div(ctx, LANES)
    base = group * LANES

    loads = [
        pltpu.make_async_copy(src, dst, load_sem.at[i])
        for i, (src, dst) in enumerate(
            [(tok_hbm, tok), (wk_hbm, wk), (wv_hbm, wv), (wq_hbm, wq),
             (wo_hbm, wo), (sk_hbm, sk), (sv_hbm, sv), (sq_hbm, sq)]
        )
    ]
    for load in loads:
        load.start()

    barrier = pltpu.get_barrier_semaphore()

    def greet(who):
        pl.semaphore_signal(
            barrier, inc=1, device_id={"ctx": who}, device_id_type=pl.DeviceIdType.MESH
        )

    for i in range(1, LANES):
        greet(base + lax.rem(me + i, LANES))
    for i in range(1, groups):
        greet(lax.rem(group + i, groups) * LANES + me)

    @pl.when(me == 0)
    def _():
        greet(lax.rem(ctx + n - 1, n))

    @pl.when(me == LANES - 1)
    def _():
        greet(lax.rem(ctx + 1, n))

    loads[0].wait()
    for r in range(0, rows, 128):
        x = tok[r:r + 128, :].astype(F32)
        normed[r:r + 128, :] = rms(x, g1_ref[...]).astype(BF16)

    edge = jnp.where((me == 0) | (me == LANES - 1), 1, 0)
    pl.semaphore_wait(barrier, LANES - 1 + groups - 1 + edge)

    loads[1].wait()
    loads[2].wait()
    copies_a = []
    for i in range(LANES):
        pair = lax.rem(me + 1 + i, LANES)
        cols = pl.ds(pl.multiple_of(pair * PAIR, PAIR), PAIR)
        x = normed[...]
        k = silu(dot(x, wk[:, cols])).astype(BF16)
        v = dot(x, wv[:, cols]).astype(BF16)
        lin_k[:, cols] = k
        lin_v[:, cols] = v
        s0 = t_dot(k[:SPAN], v[:SPAN])
        s1 = t_dot(k[SPAN:], v[SPAN:])
        for j in range(2):
            d = slice(j * DK, (j + 1) * DK)
            first_state[pair, j] = s0[d, d]
            total = (s0[d, d] + s1[d, d]).astype(BF16)
            if i < LANES - 1:
                send_a[i, j] = total
            else:
                recv_a[me, j] = total
        if i < LANES - 1:
            copy = remote(send_a.at[i], recv_a.at[me], sa.at[i], ra.at[me], base + pair)
            copy.start()
            copies_a.append(copy)

    loads[3].wait()
    for p in range(LANES):
        cols = slice(p * PAIR, (p + 1) * PAIR)
        lin_q[:, cols] = silu(dot(normed[...], wq[:, cols])).astype(BF16)

    for i in range(1, LANES):
        src = lax.rem(me + i, LANES)
        remote(recv_a.at[src], recv_a.at[src], sa.at[0], ra.at[src], base + src).wait_recv()
    whole = recv_a[0].astype(F32)
    for j in range(1, LANES):
        whole = whole + recv_a[j].astype(F32)
    send_b[...] = whole.astype(BF16)

    def to_group(d, go):
        copy = remote(
            send_b, recv_b.at[group], sb.at[d], rb.at[group],
            lax.rem(ctx + (d + 1) * LANES, n),
        )

        @pl.when(group + d + 1 < groups)
        def _():
            if go:
                copy.start()
            else:
                copy.wait_send()

    for d in range(groups - 1):
        to_group(d, True)

    row = lax.broadcasted_iota(jnp.int32, (SPAN, SPAN), 0)
    col = lax.broadcasted_iota(jnp.int32, (SPAN, SPAN), 1)
    causal = row >= col
    for h in range(H):
        cols = slice(h * DK, (h + 1) * DK)
        for c in range(rows // SPAN):
            span = slice(c * SPAN, (c + 1) * SPAN)
            v = lin_v[span, cols]
            inner = dot_t(lin_q[span, cols], lin_k[span, cols])
            inner = jnp.where(causal, inner, 0.0).astype(BF16)
            mixed[span, cols] = dot(inner, v)

    earlier[...] = jnp.zeros_like(earlier)

    @pl.loop(0, group)
    def _(g):
        remote(recv_b.at[g], recv_b.at[g], sb.at[0], rb.at[g], base + lax.rem(me + 1, LANES)).wait_recv()
        earlier[...] += recv_b[g].astype(F32)

    prefix = earlier[...]
    for j in range(LANES):
        send_c[j] = prefix.astype(BF16)
        if j < LANES - 1:
            prefix = prefix + recv_a[j].astype(F32)
    copies_c = []
    for i in range(1, LANES):
        dst = lax.rem(me + i, LANES)
        copy = remote(send_c.at[dst], recv_c.at[me], sc.at[i - 1], rc.at[me], base + dst)
        copy.start()
        copies_c.append(copy)
    recv_c[me] = send_c[me]
    for i in range(1, LANES):
        src = lax.rem(me + i, LANES)
        remote(recv_c.at[src], recv_c.at[src], sc.at[0], rc.at[src], base + src).wait_recv()

    for h in range(H):
        cols = slice(h * DK, (h + 1) * DK)
        before = recv_c[h // 2, h % 2]
        mixed[:SPAN, cols] += dot(lin_q[:SPAN, cols], before)
        later = before.astype(F32) + first_state[h // 2, h % 2]
        high = later.astype(BF16)
        low = (later - high.astype(F32)).astype(BF16)
        q = lin_q[SPAN:, cols]
        mixed[SPAN:, cols] += dot(q, high) + dot(q, low)

    for r in range(0, rows, 128):
        normed[r:r + 128, :] = rms(mixed[r:r + 128, :], gm_ref[...]).astype(BF16)
    loads[4].wait()
    for p in range(LANES):
        cols = slice(p * PAIR, (p + 1) * PAIR)
        mixed[:, cols] = tok[:, cols].astype(F32) + dot(normed[...], wo[:, cols])
    for r in range(0, rows, 128):
        normed[r:r + 128, :] = rms(mixed[r:r + 128, :], g2_ref[...]).astype(BF16)

    loads[5].wait()
    loads[6].wait()
    soft_kv[0] = dot(normed[...], sk[...]).astype(BF16)
    soft_kv[1] = dot(normed[...], sv[...]).astype(BF16)
    following = lax.rem(ctx + 1, n)
    copy_kv = [
        remote(soft_kv.at[i], prior_kv.at[i], skv.at[i], rkv.at[i], following) for i in range(2)
    ]

    @pl.when(ctx < n - 1)
    def _():
        for copy in copy_kv:
            copy.start()

    loads[7].wait()
    for p in range(LANES):
        cols = slice(p * PAIR, (p + 1) * PAIR)
        soft_q[:, cols] = dot(normed[...], sq[:, cols]).astype(BF16)

    frames = frames_ref[...]
    ones = jnp.ones((rows, DK), BF16)
    half = rows // 2
    for r in range(0, rows, half):
        span = slice(r, r + half)
        mine = jnp.transpose(jnp.broadcast_to(frames[:, span], (DK, half)))[:, :1]
        allowed = frames <= mine
        for h in range(H):
            cols = slice(h * DK, (h + 1) * DK)
            kv = slice((h // (H // KVH)) * DK, (h // (H // KVH) + 1) * DK)
            s = dot_t(soft_q[span, cols], soft_kv[0, :, kv])
            s = jnp.where(allowed, s, -1e30)
            m = jnp.max(s, axis=-1, keepdims=True)
            w = jnp.exp2((s - m) * EXP2_SCALE).astype(BF16)
            acc[h, span, :] = dot(w, jnp.concatenate([soft_kv[1, :, kv], ones], axis=1))
            peak[h, span, :] = m

    @pl.when(ctx > 0)
    def _():
        for copy in copy_kv:
            copy.wait_recv()
        for h in range(H):
            for r in range(0, rows, half):
                span = slice(r, r + half)
                cols = slice(h * DK, (h + 1) * DK)
                kv = slice((h // (H // KVH)) * DK, (h // (H // KVH) + 1) * DK)
                s = dot_t(soft_q[span, cols], prior_kv[0, :, kv])
                before_m = peak[h, span, :]
                m = jnp.maximum(before_m, jnp.max(s, axis=-1, keepdims=True))
                w = jnp.exp2((s - m) * EXP2_SCALE).astype(BF16)
                scale = jnp.exp2((before_m - m) * EXP2_SCALE)
                both = acc[h, span, :] * scale + dot(
                    w, jnp.concatenate([prior_kv[1, :, kv], ones], axis=1)
                )
                out_buf[span, cols] = (both[:, :DK] / both[:, DK:]).astype(BF16)
            pltpu.make_async_copy(out_buf.at[:, cols], out_hbm.at[:, cols], out_sem.at[h]).start()

    @pl.when(ctx == 0)
    def _():
        for h in range(H):
            cols = slice(h * DK, (h + 1) * DK)
            both = acc[h]
            out_buf[:, cols] = (both[:, :DK] / both[:, DK:]).astype(BF16)
            pltpu.make_async_copy(out_buf.at[:, cols], out_hbm.at[:, cols], out_sem.at[h]).start()

    for copy in copies_a + copies_c:
        copy.wait_send()
    for d in range(groups - 1):
        to_group(d, False)

    @pl.when(ctx < n - 1)
    def _():
        for copy in copy_kv:
            copy.wait_send()

    for h in range(H):
        cols = slice(h * DK, (h + 1) * DK)
        pltpu.make_async_copy(out_buf.at[:, cols], out_hbm.at[:, cols], out_sem.at[h]).wait()


def body(
    n,
    tokens, frames, norm_first, lin_query, lin_key, lin_value, norm_mixed, lin_out,
    norm_second, soft_query, soft_key, soft_value,
):
    rows, width = tokens.shape
    groups = n // LANES
    any_spec = pl.BlockSpec(memory_space=pl.ANY)
    vmem = pl.BlockSpec(memory_space=pltpu.VMEM)
    dma = pltpu.SemaphoreType.DMA
    state = (2, DK, DK)
    return pl.pallas_call(
        functools.partial(kernel, n),
        out_shape=jax.ShapeDtypeStruct((rows, H * DK), BF16),
        in_specs=[any_spec, vmem, vmem, vmem, vmem] + [any_spec] * 7,
        out_specs=any_spec,
        scratch_shapes=[
            pltpu.VMEM((rows, width), BF16),
            pltpu.VMEM(lin_query.shape, BF16),
            pltpu.VMEM(lin_key.shape, BF16),
            pltpu.VMEM(lin_value.shape, BF16),
            pltpu.VMEM(lin_out.shape, BF16),
            pltpu.VMEM(soft_query.shape, BF16),
            pltpu.VMEM(soft_key.shape, BF16),
            pltpu.VMEM(soft_value.shape, BF16),
            pltpu.VMEM((rows, width), BF16),
            pltpu.VMEM((rows, H * DK), BF16),
            pltpu.VMEM((rows, H * DK), BF16),
            pltpu.VMEM((rows, H * DK), BF16),
            pltpu.VMEM((rows, H * DK), F32),
            pltpu.VMEM((LANES,) + state, F32),
            pltpu.VMEM((LANES - 1,) + state, BF16),
            pltpu.VMEM((LANES,) + state, BF16),
            pltpu.VMEM(state, BF16),
            pltpu.VMEM((groups,) + state, BF16),
            pltpu.VMEM((LANES,) + state, BF16),
            pltpu.VMEM((LANES,) + state, BF16),
            pltpu.VMEM(state, F32),
            pltpu.VMEM((rows, H * DK), BF16),
            pltpu.VMEM((2, rows, KVH * DK), BF16),
            pltpu.VMEM((2, rows, KVH * DK), BF16),
            pltpu.VMEM((H, rows, 1), F32),
            pltpu.VMEM((H, rows, 2 * DK), F32),
            pltpu.VMEM((rows, H * DK), BF16),
            dma((8,)),
            dma((LANES - 1,)),
            dma((LANES,)),
            dma((groups,)),
            dma((groups,)),
            dma((LANES - 1,)),
            dma((LANES,)),
            dma((2,)),
            dma((2,)),
            dma((H,)),
        ],
        compiler_params=pltpu.CompilerParams(
            collective_id=0, has_side_effects=True, vmem_limit_bytes=56 * 2**20
        ),
    )(
        tokens,
        frames.reshape(1, rows),
        norm_first.reshape(1, width),
        norm_mixed.reshape(1, H * DK),
        norm_second.reshape(1, width),
        lin_query, lin_key, lin_value, lin_out, soft_query, soft_key, soft_value,
    )


def solution(mesh):
    n = mesh.shape["ctx"]
    return jax.shard_map(
        functools.partial(body, n),
        mesh=mesh,
        in_specs=(P(("group", "ctx"), None), P(("group", "ctx"))) + (P(),) * 10,
        out_specs=P(("group", "ctx"), None),
        check_vma=False,
    )
```

time: 172 us -> 38.6 us (0.22)
  the two profiles are of different devices: /device:TPU:26 before, /device:TPU:30 now
where the time goes in v1:
time: 38.6 us; the launch traced here: 38.4 us
  Pallas kernels  36.1 us (94%)
  local copies, waits for them, and re-layouts  2.26 us (6%)
    pallas_call x1, Pallas kernels, body(): pl.pallas_call(functools.partial(kernel, n), out_shape=jax.ShapeDtypeStru...  36.1 us
    unnamed x1, local copies, waits for them, and re-layouts  2.26 us

profile of v1, /device:TPU:30, one launch (start us, length us, event | category | flops | bytes accessed | tf_op | source)
XLA Modules:
  0.0 38.4 jit_solution(7582740654356088949)
XLA Ops:
  0.0 36.1 %shard_map.118 = bf16[512,1024]{1,0:T(8,128)(2,1)} custom-call(bf16[512,1024]{1,0:T(8,128)(2,1)} %tok_hbm.1, s32[1,512]{1,0:T(1,128)} %bitcast.7, f32[1,1024]{1,0:T(1,128)} %bitcast.4, f32[1,1024]{1,0:T(1,128)} %bitcast.5, f32[1,1024]{1,0:T(1,128)} %bitcast.6, bf16[1024,1024]{1,0:T(8,128)(2,1)} %wq_hbm.1, bf16[1024,1024]{1,0:T(8,128)(2,1)} %wk_hbm.1, ...), custom_call_target="tpu_custom_call" | custom-call | tf_op jit(solution)/shard_map/pallas_call | solution.py:310
  36.1 2.3 %copy.14 = bf16[512,1024]{1,0:T(8,128)(2,1)} copy(bf16[512,1024]{1,0:T(8,128)(2,1)} %shard_map.118) | data formatting | bytes 2097152

commit v2 on v1

--- a/solution.py
+++ b/solution.py
@@ -13,6 +13,8 @@
 KVH = 2
 SPAN = 256
 LANES = 4
+CHUNKS = H // LANES
+PART = LANES * DK
 PAIR = 2 * DK
 epsilon = 1e-05
 EXP2_SCALE = DK ** (-0.5) * math.log2(math.e)
@@ -70,15 +72,26 @@
     group = lax.div(ctx, LANES)
     base = group * LANES
 
-    loads = [
-        pltpu.make_async_copy(src, dst, load_sem.at[i])
-        for i, (src, dst) in enumerate(
-            [(tok_hbm, tok), (wk_hbm, wk), (wv_hbm, wv), (wq_hbm, wq),
-             (wo_hbm, wo), (sk_hbm, sk), (sv_hbm, sv), (sq_hbm, sq)]
-        )
+    def load(i, src, dst):
+        return pltpu.make_async_copy(src, dst, load_sem.at[i])
+
+    def part(ref, c):
+        return ref.at[:, c * PART:(c + 1) * PART]
+
+    load_tok = load(0, tok_hbm, tok)
+    load_kv = [
+        [load(1 + 2 * c, part(wk_hbm, c), part(wk, c)), load(2 + 2 * c, part(wv_hbm, c), part(wv, c))]
+        for c in range(CHUNKS)
     ]
-    for load in loads:
-        load.start()
+    load_q = load(1 + 2 * CHUNKS, wq_hbm, wq)
+    load_o = load(2 + 2 * CHUNKS, wo_hbm, wo)
+    load_soft = [
+        load(3 + 2 * CHUNKS + i, src, dst)
+        for i, (src, dst) in enumerate([(sk_hbm, sk), (sv_hbm, sv), (sq_hbm, sq)])
+    ]
+    load_tok.start()
+    for copy in load_kv[0]:
+        copy.start()
 
     barrier = pltpu.get_barrier_semaphore()
 
@@ -100,7 +113,10 @@
     def _():
         greet(lax.rem(ctx + 1, n))
 
-    loads[0].wait()
+    load_tok.wait()
+    for c in range(1, CHUNKS):
+        for copy in load_kv[c]:
+            copy.start()
     for r in range(0, rows, 128):
         x = tok[r:r + 128, :].astype(F32)
         normed[r:r + 128, :] = rms(x, g1_ref[...]).astype(BF16)
@@ -108,48 +124,41 @@
     edge = jnp.where((me == 0) | (me == LANES - 1), 1, 0)
     pl.semaphore_wait(barrier, LANES - 1 + groups - 1 + edge)
 
-    loads[1].wait()
-    loads[2].wait()
     copies_a = []
-    for i in range(LANES):
-        pair = lax.rem(me + 1 + i, LANES)
-        cols = pl.ds(pl.multiple_of(pair * PAIR, PAIR), PAIR)
-        x = normed[...]
-        k = silu(dot(x, wk[:, cols])).astype(BF16)
-        v = dot(x, wv[:, cols]).astype(BF16)
-        lin_k[:, cols] = k
-        lin_v[:, cols] = v
-        s0 = t_dot(k[:SPAN], v[:SPAN])
-        s1 = t_dot(k[SPAN:], v[SPAN:])
-        for j in range(2):
-            d = slice(j * DK, (j + 1) * DK)
-            first_state[pair, j] = s0[d, d]
-            total = (s0[d, d] + s1[d, d]).astype(BF16)
-            if i < LANES - 1:
-                send_a[i, j] = total
-            else:
-                recv_a[me, j] = total
-        if i < LANES - 1:
-            copy = remote(send_a.at[i], recv_a.at[me], sa.at[i], ra.at[me], base + pair)
+    for c in range(CHUNKS):
+        for copy in load_kv[c]:
+            copy.wait()
+        if c == 0:
+            load_q.start()
+            load_o.start()
+        for p in range(c * LANES // 2, (c + 1) * LANES // 2):
+            cols = slice(p * PAIR, (p + 1) * PAIR)
+            x = normed[...]
+            k = silu(dot(x, wk[:, cols])).astype(BF16)
+            v = dot(x, wv[:, cols]).astype(BF16)
+            lin_k[:, cols] = k
+            lin_v[:, cols] = v
+            s0 = t_dot(k[:SPAN], v[:SPAN])
+            s1 = t_dot(k[SPAN:], v[SPAN:])
+            for j in range(2):
+                h = 2 * p + j
+                d = slice(j * DK, (j + 1) * DK)
+                first_state[h] = s0[d, d]
+                send_a[c, h % LANES] = (s0[d, d] + s1[d, d]).astype(BF16)
+        recv_a[c, me] = send_a[c, me]
+        for i in range(1, LANES):
+            dst = lax.rem(me + i, LANES)
+            copy = remote(
+                send_a.at[c, dst], recv_a.at[c, me], sa.at[c, i - 1], ra.at[c, me], base + dst
+            )
             copy.start()
             copies_a.append(copy)
-
-    loads[3].wait()
-    for p in range(LANES):
-        cols = slice(p * PAIR, (p + 1) * PAIR)
-        lin_q[:, cols] = silu(dot(normed[...], wq[:, cols])).astype(BF16)
-
-    for i in range(1, LANES):
-        src = lax.rem(me + i, LANES)
-        remote(recv_a.at[src], recv_a.at[src], sa.at[0], ra.at[src], base + src).wait_recv()
-    whole = recv_a[0].astype(F32)
-    for j in range(1, LANES):
-        whole = whole + recv_a[j].astype(F32)
-    send_b[...] = whole.astype(BF16)
-
-    def to_group(d, go):
+    for copy in load_soft:
+        copy.start()
+
+    def to_group(c, d, go):
         copy = remote(
-            send_b, recv_b.at[group], sb.at[d], rb.at[group],
+            send_b.at[c], recv_b.at[c, group], sb.at[c, d], rb.at[c, group],
             lax.rem(ctx + (d + 1) * LANES, n),
         )
 
@@ -160,8 +169,25 @@
             else:
                 copy.wait_send()
 
-    for d in range(groups - 1):
-        to_group(d, True)
+    def group_total(c):
+        for i in range(1, LANES):
+            src = lax.rem(me + i, LANES)
+            remote(
+                recv_a.at[c, src], recv_a.at[c, src], sa.at[c, 0], ra.at[c, src], base + src
+            ).wait_recv()
+        whole = recv_a[c, 0].astype(F32)
+        for j in range(1, LANES):
+            whole = whole + recv_a[c, j].astype(F32)
+        send_b[c] = whole.astype(BF16)
+        for d in range(groups - 1):
+            to_group(c, d, True)
+
+    load_q.wait()
+    for c in range(CHUNKS):
+        group_total(c)
+        for p in range(c * LANES // 2, (c + 1) * LANES // 2):
+            cols = slice(p * PAIR, (p + 1) * PAIR)
+            lin_q[:, cols] = silu(dot(normed[...], wq[:, cols])).astype(BF16)
 
     row = lax.broadcasted_iota(jnp.int32, (SPAN, SPAN), 0)
     col = lax.broadcasted_iota(jnp.int32, (SPAN, SPAN), 1)
@@ -175,50 +201,60 @@
             inner = jnp.where(causal, inner, 0.0).astype(BF16)
             mixed[span, cols] = dot(inner, v)
 
-    earlier[...] = jnp.zeros_like(earlier)
-
-    @pl.loop(0, group)
-    def _(g):
-        remote(recv_b.at[g], recv_b.at[g], sb.at[0], rb.at[g], base + lax.rem(me + 1, LANES)).wait_recv()
-        earlier[...] += recv_b[g].astype(F32)
-
-    prefix = earlier[...]
-    for j in range(LANES):
-        send_c[j] = prefix.astype(BF16)
-        if j < LANES - 1:
-            prefix = prefix + recv_a[j].astype(F32)
     copies_c = []
-    for i in range(1, LANES):
-        dst = lax.rem(me + i, LANES)
-        copy = remote(send_c.at[dst], recv_c.at[me], sc.at[i - 1], rc.at[me], base + dst)
-        copy.start()
-        copies_c.append(copy)
-    recv_c[me] = send_c[me]
-    for i in range(1, LANES):
-        src = lax.rem(me + i, LANES)
-        remote(recv_c.at[src], recv_c.at[src], sc.at[0], rc.at[src], base + src).wait_recv()
-
-    for h in range(H):
-        cols = slice(h * DK, (h + 1) * DK)
-        before = recv_c[h // 2, h % 2]
-        mixed[:SPAN, cols] += dot(lin_q[:SPAN, cols], before)
-        later = before.astype(F32) + first_state[h // 2, h % 2]
-        high = later.astype(BF16)
-        low = (later - high.astype(F32)).astype(BF16)
-        q = lin_q[SPAN:, cols]
-        mixed[SPAN:, cols] += dot(q, high) + dot(q, low)
+    for c in range(CHUNKS):
+        earlier[...] = jnp.zeros_like(earlier)
+
+        @pl.loop(0, group)
+        def _(g):
+            remote(
+                recv_b.at[c, g], recv_b.at[c, g], sb.at[c, 0], rb.at[c, g],
+                base + lax.rem(me + 1, LANES),
+            ).wait_recv()
+            earlier[...] += recv_b[c, g].astype(F32)
+
+        prefix = earlier[...]
+        for j in range(LANES):
+            send_c[c, j] = prefix.astype(BF16)
+            if j < LANES - 1:
+                prefix = prefix + recv_a[c, j].astype(F32)
+        for i in range(1, LANES):
+            dst = lax.rem(me + i, LANES)
+            copy = remote(
+                send_c.at[c, dst], recv_c.at[c, me], sc.at[c, i - 1], rc.at[c, me], base + dst
+            )
+            copy.start()
+            copies_c.append(copy)
+        recv_c[c, me] = send_c[c, me]
+
+    for c in range(CHUNKS):
+        for i in range(1, LANES):
+            src = lax.rem(me + i, LANES)
+            remote(
+                recv_c.at[c, src], recv_c.at[c, src], sc.at[c, 0], rc.at[c, src], base + src
+            ).wait_recv()
+        for j in range(LANES):
+            h = c * LANES + j
+            cols = slice(h * DK, (h + 1) * DK)
+            before = recv_c[c, j]
+            mixed[:SPAN, cols] += dot(lin_q[:SPAN, cols], before)
+            later = before.astype(F32) + first_state[h]
+            high = later.astype(BF16)
+            low = (later - high.astype(F32)).astype(BF16)
+            q = lin_q[SPAN:, cols]
+            mixed[SPAN:, cols] += dot(q, high) + dot(q, low)
 
     for r in range(0, rows, 128):
         normed[r:r + 128, :] = rms(mixed[r:r + 128, :], gm_ref[...]).astype(BF16)
-    loads[4].wait()
+    load_o.wait()
     for p in range(LANES):
         cols = slice(p * PAIR, (p + 1) * PAIR)
         mixed[:, cols] = tok[:, cols].astype(F32) + dot(normed[...], wo[:, cols])
     for r in range(0, rows, 128):
         normed[r:r + 128, :] = rms(mixed[r:r + 128, :], g2_ref[...]).astype(BF16)
 
-    loads[5].wait()
-    loads[6].wait()
+    load_soft[0].wait()
+    load_soft[1].wait()
     soft_kv[0] = dot(normed[...], sk[...]).astype(BF16)
     soft_kv[1] = dot(normed[...], sv[...]).astype(BF16)
     following = lax.rem(ctx + 1, n)
@@ -231,7 +267,7 @@
         for copy in copy_kv:
             copy.start()
 
-    loads[7].wait()
+    load_soft[2].wait()
     for p in range(LANES):
         cols = slice(p * PAIR, (p + 1) * PAIR)
         soft_q[:, cols] = dot(normed[...], sq[:, cols]).astype(BF16)
@@ -283,8 +319,9 @@
 
     for copy in copies_a + copies_c:
         copy.wait_send()
-    for d in range(groups - 1):
-        to_group(d, False)
+    for c in range(CHUNKS):
+        for d in range(groups - 1):
+            to_group(c, d, False)
 
     @pl.when(ctx < n - 1)
     def _():
@@ -306,7 +343,7 @@
     any_spec = pl.BlockSpec(memory_space=pl.ANY)
     vmem = pl.BlockSpec(memory_space=pltpu.VMEM)
     dma = pltpu.SemaphoreType.DMA
-    state = (2, DK, DK)
+    state = (DK, DK)
     return pl.pallas_call(
         functools.partial(kernel, n),
         out_shape=jax.ShapeDtypeStruct((rows, H * DK), BF16),
@@ -326,13 +363,13 @@
             pltpu.VMEM((rows, H * DK), BF16),
             pltpu.VMEM((rows, H * DK), BF16),
             pltpu.VMEM((rows, H * DK), F32),
-            pltpu.VMEM((LANES,) + state, F32),
-            pltpu.VMEM((LANES - 1,) + state, BF16),
-            pltpu.VMEM((LANES,) + state, BF16),
-            pltpu.VMEM(state, BF16),
-            pltpu.VMEM((groups,) + state, BF16),
-            pltpu.VMEM((LANES,) + state, BF16),
-            pltpu.VMEM((LANES,) + state, BF16),
+            pltpu.VMEM((H,) + state, F32),
+            pltpu.VMEM((CHUNKS, LANES) + state, BF16),
+            pltpu.VMEM((CHUNKS, LANES) + state, BF16),
+            pltpu.VMEM((CHUNKS,) + state, BF16),
+            pltpu.VMEM((CHUNKS, groups) + state, BF16),
+            pltpu.VMEM((CHUNKS, LANES) + state, BF16),
+            pltpu.VMEM((CHUNKS, LANES) + state, BF16),
             pltpu.VMEM(state, F32),
             pltpu.VMEM((rows, H * DK), BF16),
             pltpu.VMEM((2, rows, KVH * DK), BF16),
@@ -340,13 +377,13 @@
             pltpu.VMEM((H, rows, 1), F32),
             pltpu.VMEM((H, rows, 2 * DK), F32),
             pltpu.VMEM((rows, H * DK), BF16),
-            dma((8,)),
-            dma((LANES - 1,)),
-            dma((LANES,)),
-            dma((groups,)),
-            dma((groups,)),
-            dma((LANES - 1,)),
-            dma((LANES,)),
+            dma((6 + 2 * CHUNKS,)),
+            dma((CHUNKS, LANES - 1)),
+            dma((CHUNKS, LANES)),
+            dma((CHUNKS, groups)),
+            dma((CHUNKS, groups)),
+            dma((CHUNKS, LANES - 1)),
+            dma((CHUNKS, LANES)),
             dma((2,)),
             dma((2,)),
             dma((H,)),

time: 38.6 us -> 36.9 us (0.956)
  the two profiles are of different devices: /device:TPU:30 before, /device:TPU:26 now
where the time goes in v2:
time: 36.9 us; the launch traced here: 36.7 us
  Pallas kernels  34.4 us (93%)
  local copies, waits for them, and re-layouts  2.26 us (6%)
    pallas_call x1, Pallas kernels, body(): pl.pallas_call(functools.partial(kernel, n), out_shape=jax.ShapeDtypeStru...  34.4 us
    unnamed x1, local copies, waits for them, and re-layouts  2.26 us

profile of v2, /device:TPU:26, one launch (start us, length us, event | category | flops | bytes accessed | tf_op | source)
XLA Modules:
  0.0 36.7 jit_solution(16601287882317479743)
XLA Ops:
  0.0 34.4 %shard_map.118 = bf16[512,1024]{1,0:T(8,128)(2,1)} custom-call(bf16[512,1024]{1,0:T(8,128)(2,1)} %tok_hbm.1, s32[1,512]{1,0:T(1,128)} %bitcast.7, f32[1,1024]{1,0:T(1,128)} %bitcast.4, f32[1,1024]{1,0:T(1,128)} %bitcast.5, f32[1,1024]{1,0:T(1,128)} %bitcast.6, bf16[1024,1024]{1,0:T(8,128)(2,1)} %wq_hbm.1, bf16[1024,1024]{1,0:T(8,128)(2,1)} %wk_hbm.1, ...), custom_call_target="tpu_custom_call" | custom-call | tf_op jit(solution)/shard_map/pallas_call | solution.py:347
  34.4 2.3 %copy.14 = bf16[512,1024]{1,0:T(8,128)(2,1)} copy(bf16[512,1024]{1,0:T(8,128)(2,1)} %shard_map.118) | data formatting | bytes 2097152

commit v3 on v2

--- a/solution.py
+++ b/solution.py
@@ -120,9 +120,6 @@
     for r in range(0, rows, 128):
         x = tok[r:r + 128, :].astype(F32)
         normed[r:r + 128, :] = rms(x, g1_ref[...]).astype(BF16)
-
-    edge = jnp.where((me == 0) | (me == LANES - 1), 1, 0)
-    pl.semaphore_wait(barrier, LANES - 1 + groups - 1 + edge)
 
     copies_a = []
     for c in range(CHUNKS):
@@ -145,6 +142,9 @@
                 d = slice(j * DK, (j + 1) * DK)
                 first_state[h] = s0[d, d]
                 send_a[c, h % LANES] = (s0[d, d] + s1[d, d]).astype(BF16)
+        if c == 0:
+            edge = jnp.where((me == 0) | (me == LANES - 1), 1, 0)
+            pl.semaphore_wait(barrier, LANES - 1 + groups - 1 + edge)
         recv_a[c, me] = send_a[c, me]
         for i in range(1, LANES):
             dst = lax.rem(me + i, LANES)

time: 36.9 us -> 35.7 us (0.967)
  Pallas kernels: 34.4 us -> 33.2 us
    pallas_call x1, Pallas kernels: 34.4 us -> 33.2 us  [body(): pl.pallas_call(functools.partial(kernel, n), out_shape=jax.ShapeDtypeStru...]
where the time goes in v3:
time: 35.7 us; the launch traced here: 35.5 us
  Pallas kernels  33.2 us (93%)
  local copies, waits for them, and re-layouts  2.26 us (6%)
    pallas_call x1, Pallas kernels, body(): pl.pallas_call(functools.partial(kernel, n), out_shape=jax.ShapeDtypeStru...  33.2 us
    unnamed x1, local copies, waits for them, and re-layouts  2.26 us

profile of v3, /device:TPU:26, one launch (start us, length us, event | category | flops | bytes accessed | tf_op | source)
XLA Modules:
  0.0 35.5 jit_solution(12609369724294756425)
XLA Ops:
  0.0 33.2 %shard_map.118 = bf16[512,1024]{1,0:T(8,128)(2,1)} custom-call(bf16[512,1024]{1,0:T(8,128)(2,1)} %tok_hbm.1, s32[1,512]{1,0:T(1,128)} %bitcast.7, f32[1,1024]{1,0:T(1,128)} %bitcast.4, f32[1,1024]{1,0:T(1,128)} %bitcast.5, f32[1,1024]{1,0:T(1,128)} %bitcast.6, bf16[1024,1024]{1,0:T(8,128)(2,1)} %wq_hbm.1, bf16[1024,1024]{1,0:T(8,128)(2,1)} %wk_hbm.1, ...), custom_call_target="tpu_custom_call" | custom-call | tf_op jit(solution)/shard_map/pallas_call | solution.py:347
  33.2 2.3 %copy.14 = bf16[512,1024]{1,0:T(8,128)(2,1)} copy(bf16[512,1024]{1,0:T(8,128)(2,1)} %shard_map.118) | data formatting | bytes 2097152
